TPU v7x, 128 devices: a whole 4x4x4 slice. The times are simulated.
128 devices in a mesh: ty: 8 (over y, core), tx: 16 (over z, x).
Axes of the slice: x: 4, y: 4, z: 4, core: 2. Of those that a mesh axis runs over, the one named last changes fastest.
Arguments:
- covariates: bfloat16 [262144, 512], P(('ty', 'tx')), may hold values from -24 to 24
- w_in: bfloat16 [512, 2048], replicated, may hold values from -0.25 to 0.25
- b_in: float32 [2048], replicated, may hold values from -3 to 3
- w_out: bfloat16 [2048, 128], replicated, may hold values from -0.125 to 0.125
- b_out: float32 [128], replicated, may hold values from -2 to 2
- owner: int32 [262144, 1], P(('ty', 'tx')), may hold values from 0 to 127; in each aligned block of 2048 rows (0 to 2047, 2048 to 4095, ...) at most 32 rows name the same one
- land_cell: int32 [262144], P(('ty', 'tx')), may hold values from 0 to 2047
- row_taps: float32 [128, 9], replicated, may hold values from 0.2 to 1
- col_taps: float32 [128, 9], replicated, may hold values from 0.2 to 1
- rate: float32 [128], replicated, may hold values from 0.2 to 1.5
- capacity: float32 [128], replicated, may hold values from 0.5 to 4
- observed: int32 [128, 2048, 128], P('ty', 'tx'), may hold values from 0 to 2
- surveyed: int32 [128, 2048], P('ty', 'tx'), may hold values 0 or 1
Outputs:
- density: float32 [128, 2048, 128], P('ty', 'tx')
- grad_w_in: float32 [512, 2048], P(('ty', 'tx'))
- grad_w_out: float32 [2048, 128], P(('ty', 'tx'))
Inputs may be any that keep to these rules, and one draw needn't show every extreme that they name: `owner`: among the land cells of one device, no tile owns more than 32, and some tile owns exactly 32.
All inputs are finite; a program needn't handle non-finite values. No bound on the sum of `surveyed` on one device may be relied on, other than what follows from the above.
Results may differ from a plain program's by a relative error of at most 0.0017.
Values may be sent and summed in bfloat16 or wider, within the bound.
No kernel may reach another device: no remote copies, remote signals or barrier semaphores. Data moves between devices by JAX's collectives and lax.ppermute only.
A program may use at most 128 MiB of HBM per device.

v0:
```python
import math

import jax
import jax.numpy as jnp
from jax import lax
from jax.sharding import PartitionSpec as P

STEPS = 4


def with_halo(cells, sides, width):
    for axis, dim in sides:
        count = lax.axis_size(axis)
        ends = count - 1
        head = lax.slice_in_dim(cells, 0, width, axis=dim)
        tail = lax.slice_in_dim(cells, cells.shape[dim] - width, cells.shape[dim], axis=dim)
        cells = jnp.concatenate(
            [
                lax.ppermute(tail, axis, [(i, (i + 1) % count) for i in range(ends)]),
                cells,
                lax.ppermute(head, axis, [((i + 1) % count, i) for i in range(ends)]),
            ],
            axis=dim,
        )
    return cells


def normalize(taps):
    return taps / jnp.sum(taps, axis=1, keepdims=True)


def disperse_valid(padded, taps_y, taps_x):
    height = padded.shape[0] - 8
    width_out = padded.shape[1] - 8
    partial_rows = taps_y[:, 0] * padded[0:height]
    for offset in range(1, 9):
        partial_rows = partial_rows + taps_y[:, offset] * padded[offset : offset + height]
    result = taps_x[:, 0] * partial_rows[:, 0:width_out]
    for offset in range(1, 9):
        result = result + taps_x[:, offset] * partial_rows[:, offset : offset + width_out]
    return result


def silu_slope(value):
    sigmoid_v = jax.nn.sigmoid(value)
    return sigmoid_v + value * sigmoid_v * (1.0 - sigmoid_v)


def local(
    covariates,
    w_in,
    b_in,
    w_out,
    b_out,
    owner,
    land_cell,
    row_taps,
    col_taps,
    rate,
    capacity,
    observed,
    surveyed,
):
    row_count = covariates.shape[0]
    tiles_y = lax.axis_size("ty")
    tiles_x = lax.axis_size("tx")
    devices = tiles_y * tiles_x
    slot_count = 2 * row_count // devices
    height, tile_width, species = observed.shape
    cell_count = height * tile_width
    preact = jnp.dot(covariates, w_in, preferred_element_type=jnp.float32) + b_in
    hidden = jax.nn.silu(preact).astype(jnp.bfloat16)
    log_rate = jnp.dot(hidden, w_out, preferred_element_type=jnp.float32) + b_out
    intensity = jnp.exp(log_rate)
    sent = intensity.astype(jnp.bfloat16)
    owner_rows = owner[:, 0]
    onehot = (owner_rows[:, None] == jnp.arange(devices, dtype=jnp.int32)[None, :]).astype(
        jnp.int32
    )
    before = jnp.cumsum(onehot, axis=0) - onehot
    slot_idx = jnp.sum(before * onehot, axis=1)
    flat_slot = owner_rows * slot_count + slot_idx
    send_values = jnp.zeros((devices * slot_count, species), jnp.bfloat16).at[flat_slot].set(sent)
    send_cells = (
        jnp.full((devices * slot_count,), cell_count, jnp.int32).at[flat_slot].set(land_cell)
    )
    got_values, got_cells = (
        lax.all_to_all(
            send_values.reshape(devices, slot_count, species),
            ("ty", "tx"),
            split_axis=0,
            concat_axis=0,
            tiled=True,
        ),
        lax.all_to_all(
            send_cells.reshape(devices, slot_count),
            ("ty", "tx"),
            split_axis=0,
            concat_axis=0,
            tiled=True,
        ),
    )
    cell_list = got_cells.reshape(-1)
    start_field = (
        jnp.zeros((cell_count, species), jnp.float32)
        .at[cell_list]
        .add(got_values.reshape(-1, species).astype(jnp.float32), mode="drop")
    )
    field = 0.1 + start_field.reshape(height, tile_width, species)
    taps_y = normalize(row_taps)
    taps_x = normalize(col_taps)
    back_y = taps_y[:, ::-1]
    back_x = taps_x[:, ::-1]
    scale = 1.0 / math.sqrt(row_count * devices)
    stored = []
    for step in range(STEPS):
        padded = with_halo(field, (("ty", 0), ("tx", 1)), 4)
        mid_value = disperse_valid(padded, taps_y, taps_x)
        stored.append(mid_value)
        field = mid_value * (1.0 + rate) / (1.0 + rate * mid_value / capacity)
    grad_field = (
        surveyed[:, :, None].astype(jnp.float32)
        * (1.0 - observed.astype(jnp.float32) / field)
        * scale
    )
    for step in range(STEPS - 1, -1, -1):
        mid_value = stored[step]
        denom = 1.0 + rate * mid_value / capacity
        grad_mid = grad_field * (1.0 + rate) / (denom * denom)
        padded = with_halo(grad_mid.astype(jnp.bfloat16), (("ty", 0), ("tx", 1)), 4).astype(
            grad_mid.dtype
        )
        grad_field = disperse_valid(padded, back_y, back_x)
    back_values = jnp.take(
        grad_field.reshape(cell_count, species), cell_list, axis=0, mode="fill", fill_value=0.0
    ).astype(jnp.bfloat16)
    home_values = lax.all_to_all(
        back_values.reshape(devices, slot_count, species),
        ("ty", "tx"),
        split_axis=0,
        concat_axis=0,
        tiled=True,
    )
    returned = home_values.reshape(devices * slot_count, species)[flat_slot]
    dlog = (returned.astype(jnp.float32) * intensity).astype(jnp.bfloat16)
    dhidden = lax.dot_general(
        dlog, w_out, (((1,), (1,)), ((), ())), preferred_element_type=jnp.float32
    )
    dpre = (dhidden * silu_slope(preact)).astype(jnp.bfloat16)
    piece = covariates
    grad_w_in = lax.psum_scatter(
        lax.dot_general(piece, dpre, (((0,), (0,)), ((), ())), preferred_element_type=jnp.float32),
        ("ty", "tx"),
        scatter_dimension=0,
        tiled=True,
    )
    piece = hidden
    grad_w_out = lax.psum_scatter(
        lax.dot_general(piece, dlog, (((0,), (0,)), ((), ())), preferred_element_type=jnp.float32),
        ("ty", "tx"),
        scatter_dimension=0,
        tiled=True,
    )
    return (field, grad_w_in, grad_w_out)


def solution(mesh):
    in_specs = (
        P(("ty", "tx"), None),
        P(),
        P(),
        P(),
        P(),
        P(("ty", "tx"), None),
        P(("ty", "tx")),
        P(),
        P(),
        P(),
        P(),
        P("ty", "tx", None),
        P("ty", "tx"),
    )
    out_specs = (P("ty", "tx", None), P(("ty", "tx"), None), P(("ty", "tx"), None))
    return jax.shard_map(local, mesh=mesh, in_specs=in_specs, out_specs=out_specs, check_vma=False)
```

profile of v0, /device:TPU:0, one launch (start us, length us, event | category | flops | bytes accessed | tf_op | source)
XLA Modules:
  0.0 1142.0 jit_solution(3777423167045034763)
XLA Ops:
  10.0 8.2 scatter_custom_fusion
  18.9 11.1 all-to-all-start
  30.1 10.9 fusion
  44.3 6.8 scatter_custom_fusion.1
  51.1 10.5 all-to-all-start.1
  63.0 17.1 %all-to-all-done.1 = bf16[128,32,128]{2,1,0:T(8,128)(2,1)} async-done(((bf16[128,32,128]{2,1,0:T(8,128)(2,1)}), bf16[128,32,128]{2,1,0:T(8,128)(2,1)}, u32[]{:S(2)}, u32[]{:S(2)}) %all-to-all-start.1) | async-done | bytes 1048608 | tf_op jit(solution)/shard_map/all_to_all | solution.py:88
  80.2 23.0 %scatter_custom_fusion.2 = f32[2048,128]{1,0:T(8,128)S(1)} fusion(s32[4096]{0:T(1024)S(1)} %bitcast.86, bf16[4096,128]{1,0:T(8,128)(2,1)} %bitcast.40, f32[]{:T(128)} %constant.11.clone.1), kind=kCustom, calls=%fused_computation.12 | custom fusion | flops 1048576 | bytes 2097156 | tf_op jit(solution)/shard_map/scatter-add | solution.py:107
  124.4 5.5 collective-permute-done.5
  140.6 5.2 collective-permute-start.8
  150.3 5.1 collective-permute-start.10
  163.5 5.4 collective-permute-start.12
  178.7 4.3 collective-permute-done.15
  186.8 5.5 collective-permute-start.16
  208.3 4.3 collective-permute-start.20
  228.4 4.3 collective-permute-start.24
  248.5 4.3 collective-permute-start.28
  268.4 15.0 %gather_fusion = bf16[4096,128]{1,0:T(8,128)(2,1)} fusion(bf16[2048,128]{1,0:T(8,128)(2,1)S(1)} %bitcast.75, s32[4096]{0:T(1024)S(1)} %broadcast_clamp_fusion), kind=kCustom, calls=%fused_computation | custom fusion | bytes 2113536 | tf_op jit(solution)/shard_map/jit(_take)/gather | solution.py:134
  286.9 11.9 %all-to-all-start.2 = ((bf16[128,32,128]{2,1,0:T(8,128)(2,1)}), bf16[128,32,128]{2,1,0:T(8,128)(2,1)S(1)}, u32[]{:S(2)}, u32[]{:S(2)}) async-start(bf16[128,32,128]{2,1,0:T(8,128)(2,1)} %select_convert_fusion), calls=%async_computation.2 | async-start | bytes 2097152 | tf_op jit(solution)/shard_map/all_to_all | solution.py:137
  299.3 18.6 %all-to-all-done.2 = bf16[128,32,128]{2,1,0:T(8,128)(2,1)S(1)} async-done(((bf16[128,32,128]{2,1,0:T(8,128)(2,1)}), bf16[128,32,128]{2,1,0:T(8,128)(2,1)S(1)}, u32[]{:S(2)}, u32[]{:S(2)}) %all-to-all-start.2) | async-done | bytes 1048608 | tf_op jit(solution)/shard_map/all_to_all | solution.py:137
  317.9 8.0 gather_fusion.1
  325.9 18.7 %convolution_bitcast_fusion = f32[512,2048]{0,1:T(8,128)} fusion(bf16[2048,512]{1,0:T(8,128)(2,1)S(1)} %copy-done, f32[2048,2048]{1,0:T(8,128)} %get-tuple-element.73, bf16[2048,128]{1,0:T(8,128)(2,1)} %param.16, f32[2048]{0:T(1024)S(1)} %copy-done.13, f32[2048,128]{1,0:T(8,128)} %copy-done.2, bf16[2048,128]{1,0:T(8,128)(2,1)} %gather_fusion.1), kind=kOutput, calls=%fused_computation.9 | convolution fusion | flops 5411438592 | bytes 25174016 | tf_op jit(solution)/shard_map/dot_general | solution.py:152
  345.8 7.2 fusion.153
  355.5 139.0 %all-reduce.3.cloned.1.call-done = f32[512,2048]{0,1:T(8,128)} async-done(((f32[512,2048]{0,1:T(8,128)}), f32[512,2048]{0,1:T(8,128)}) %all-reduce.3.cloned.1.call-update) | async-done | bytes 4194320
  497.0 638.0 %reduce-scatter.3.cloned.1.call-done = f32[16,128]{1,0:T(8,128)} async-done(((f32[2048,128]{1,0:T(8,128)}), f32[16,128]{1,0:T(8,128)}) %reduce-scatter.3.cloned.1.call-update) | async-done | bytes 8208 | tf_op jit(solution)/shard_map/reduce_scatter | solution.py:158
  (160 shorter events, 139.0 us)
Async XLA Ops:
  18.9 32.2 %all-to-all-start = ((s32[128,1,32]{2,1,0:T(1,128)}), s32[128,1,32]{2,1,0:T(1,128)S(1)}, u32[]{:S(2)}, u32[]{:S(2)}) async-start(s32[128,1,32]{2,1,0:T(1,128)} %bitcast.9), calls=%async_computation | async-start | bytes 131072 | tf_op jit(solution)/shard_map/all_to_all | solution.py:95
  51.1 29.1 %all-to-all-start.1 = ((bf16[128,32,128]{2,1,0:T(8,128)(2,1)}), bf16[128,32,128]{2,1,0:T(8,128)(2,1)}, u32[]{:S(2)}, u32[]{:S(2)}) async-start(bf16[128,32,128]{2,1,0:T(8,128)(2,1)} %bitcast.80), calls=%async_computation.1 | async-start | bytes 2097152 | tf_op jit(solution)/shard_map/all_to_all | solution.py:88
  111.4 6.0 collective-permute-start.3
  123.1 6.8 collective-permute-start.5
  132.6 6.0 collective-permute-start.7
  140.6 6.6 collective-permute-start.8
  150.3 6.8 collective-permute-start.10
  155.4 6.0 collective-permute-start.11
  163.5 6.7 collective-permute-start.12
  173.2 5.5 collective-permute-start.14
  177.0 6.0 collective-permute-start.15
  186.8 7.0 collective-permute-start.16
  200.3 5.7 collective-permute-start.19
  208.3 5.6 collective-permute-start.20
  220.4 5.7 collective-permute-start.23
  228.4 5.6 collective-permute-start.24
  236.5 5.5 collective-permute-start.26
  240.5 5.7 collective-permute-start.27
  248.5 5.6 collective-permute-start.28
  256.6 5.5 collective-permute-start.30
  260.7 5.7 collective-permute-start.31
  286.9 30.9 %all-to-all-start.2 = ((bf16[128,32,128]{2,1,0:T(8,128)(2,1)}), bf16[128,32,128]{2,1,0:T(8,128)(2,1)S(1)}, u32[]{:S(2)}, u32[]{:S(2)}) async-start(bf16[128,32,128]{2,1,0:T(8,128)(2,1)} %select_convert_fusion), calls=%async_computation.2 | async-start | bytes 2097152 | tf_op jit(solution)/shard_map/all_to_all | solution.py:137
  298.8 195.6 %all-reduce.3.cloned.1.call-start = ((), (), s32[]{:S(2)}) async-start(), calls=%async_computation.5 | async-start | bytes 8388608
  344.6 790.3 %reduce-scatter.3.cloned.1.call-start = ((), (), s32[]{:S(2)}) async-start(), calls=%async_computation.4 | async-start | bytes 1056768 | tf_op jit(solution)/shard_map/reduce_scatter | solution.py:158
  (28 other events, 186.8 us)
Sparse Core Ops, SparseCore 0:
  344.8 149.6 all-reduce.2
  497.4 637.5 reduce-scatter.2
where the time goes:
time: 1150 us; the launch traced here: 1140 us
  waiting for transfers between devices  872 us (76%)
  starting transfers between devices  121 us (11%)
  other arithmetic  54.6 us (5%)
  local copies, waits for them, and re-layouts  40.7 us (4%)
  matrix products  39.1 us (3%)
  between operations  15 us (1%)
    reduce_scatter x1, waiting for transfers between devices, local(): lax.psum_scatter(lax.dot_general(piece, dlog, (((0,), (0,)), ((), ())), p...  638 us
    unnamed x3, waiting for transfers between devices  139 us
    ppermute x16, starting transfers between devices, with_halo(): lax.ppermute(tail, axis, [(i, (i + 1) % count) for i in range(ends)])  65.8 us
    ppermute x16, waiting for transfers between devices, with_halo(): lax.ppermute(head, axis, [((i + 1) % count, i) for i in range(ends)])  55.4 us
    scatter-add x1, other arithmetic, local(): start_field = jnp.zeros((cell_count, species), jnp.float32).at[cell_list]...  23 us
  transfers between devices with their start and end apart: 37, of which 28 were waited for; matrix products, arithmetic and copies ran while one was open for 3% of the time, Pallas kernels for 0%

commit v1 on v0

v1 whole, which is shorter than its diff:
```python
import math

import jax
import jax.numpy as jnp
from jax import lax
from jax.sharding import Mesh
from jax.sharding import PartitionSpec as P

STEPS = 4
REACH = 4
TY = ("y", "core")
TX = ("z", "x")
ALL = TY + TX
F32 = jnp.float32
BF16 = jnp.bfloat16


def shift(cells, axes, count, forward):
    pairs = [(i, i + 1) for i in range(count - 1)]
    if not forward:
        pairs = [(b, a) for a, b in pairs]
    return lax.ppermute(cells, axes, pairs)


def with_halo(cells, width, tiles_y, tiles_x):
    for axes, count, dim in ((TY, tiles_y, 0), (TX, tiles_x, 1)):
        size = cells.shape[dim]
        head = lax.slice_in_dim(cells, 0, width, axis=dim).astype(BF16)
        tail = lax.slice_in_dim(cells, size - width, size, axis=dim).astype(BF16)
        cells = jnp.concatenate(
            [
                shift(tail, axes, count, True).astype(cells.dtype),
                cells,
                shift(head, axes, count, False).astype(cells.dtype),
            ],
            axis=dim,
        )
    return cells


def normalize(taps):
    return taps / jnp.sum(taps, axis=1, keepdims=True)


def disperse_valid(padded, taps_y, taps_x):
    height = padded.shape[0] - 8
    width_out = padded.shape[1] - 8
    partial_rows = taps_y[:, 0] * padded[0:height]
    for offset in range(1, 9):
        partial_rows = partial_rows + taps_y[:, offset] * padded[offset : offset + height]
    result = taps_x[:, 0] * partial_rows[:, 0:width_out]
    for offset in range(1, 9):
        result = result + taps_x[:, offset] * partial_rows[:, offset : offset + width_out]
    return result


def silu_slope(value):
    sigmoid_v = jax.nn.sigmoid(value)
    return sigmoid_v + value * sigmoid_v * (1.0 - sigmoid_v)


def crop(cells, margin):
    return cells[margin : cells.shape[0] - margin, margin : cells.shape[1] - margin]


def reduce_scatter(part):
    n_y = lax.axis_size("y")
    peers = n_y * lax.axis_size("z") * lax.axis_size("x")
    rows, cols = part.shape
    parts = part.reshape(n_y, 2, rows // n_y // 2, cols)
    core = lax.axis_index("core")
    mine = lax.dynamic_index_in_dim(parts, core, 1, keepdims=False)
    other = lax.dynamic_index_in_dim(parts, 1 - core, 1, keepdims=False)
    both = mine + lax.ppermute(other, "core", [(0, 1), (1, 0)])
    both = both.reshape(peers, rows // peers // 2, cols)
    return jnp.sum(lax.all_to_all(both, ("y", "z", "x"), 0, 0), axis=0)


def local(
    covariates,
    w_in,
    b_in,
    w_out,
    b_out,
    owner,
    land_cell,
    row_taps,
    col_taps,
    rate,
    capacity,
    observed,
    surveyed,
):
    row_count = covariates.shape[0]
    tiles_y = lax.axis_size("y") * lax.axis_size("core")
    tiles_x = lax.axis_size("z") * lax.axis_size("x")
    devices = tiles_y * tiles_x
    slot_count = 2 * row_count // devices
    slots = devices * slot_count
    height, tile_width, species = observed.shape
    cell_count = height * tile_width
    preact = jnp.dot(covariates, w_in, preferred_element_type=F32) + b_in
    hidden = jax.nn.silu(preact).astype(BF16)
    log_rate = jnp.dot(hidden, w_out, preferred_element_type=F32) + b_out
    intensity = jnp.exp(log_rate)
    sent = intensity.astype(BF16)

    owner_rows = owner[:, 0]
    owner_hot = owner_rows[:, None] == jnp.arange(devices, dtype=jnp.int32)[None, :]
    row_ids = jnp.arange(row_count, dtype=jnp.int32)
    earlier = (row_ids[None, :] < row_ids[:, None]).astype(BF16)
    before = jnp.dot(earlier, owner_hot.astype(BF16), preferred_element_type=F32)
    slot_idx = jnp.sum(jnp.where(owner_hot, before, 0.0), axis=1).astype(jnp.int32)
    flat_slot = owner_rows * slot_count + slot_idx

    slot_ids = jnp.arange(slots, dtype=jnp.int32)
    pack = (flat_slot[None, :] == slot_ids[:, None]).astype(BF16)
    send_values = jnp.dot(pack, sent, preferred_element_type=F32).astype(BF16)
    slot_hot = slot_idx[:, None] == jnp.arange(slot_count, dtype=jnp.int32)[None, :]
    place_row = (land_cell // tile_width + 1).astype(F32)[:, None]
    place_col = (land_cell % tile_width).astype(F32)[:, None]
    places = jnp.concatenate(
        [jnp.where(slot_hot, place_row, 0.0), jnp.where(slot_hot, place_col, 0.0)], axis=1
    ).astype(BF16)
    table = lax.dot_general(
        owner_hot.astype(BF16), places, (((0,), (0,)), ((), ())), preferred_element_type=F32
    ).astype(BF16)
    table = jnp.pad(table[:, None, :], ((0, 0), (0, 7), (0, species - 2 * slot_count)))
    send = jnp.concatenate([send_values.reshape(devices, slot_count, species), table], axis=1)
    got = lax.all_to_all(send, ALL, split_axis=0, concat_axis=0, tiled=True)
    got_values = got[:, :slot_count].reshape(slots, species)
    got_row = got[:, slot_count, :slot_count].astype(jnp.int32)
    got_col = got[:, slot_count, slot_count : 2 * slot_count].astype(jnp.int32)
    cell_list = jnp.where(got_row > 0, (got_row - 1) * tile_width + got_col, -1).reshape(-1)
    cell_ids = jnp.arange(cell_count, dtype=jnp.int32)
    place = (cell_list[None, :] == cell_ids[:, None]).astype(BF16)
    start_field = jnp.dot(place, got_values, preferred_element_type=F32)
    start_field = start_field.reshape(height, tile_width, species)

    taps_y = normalize(row_taps)
    taps_x = normalize(col_taps)
    back_y = taps_y[:, ::-1]
    back_x = taps_x[:, ::-1]
    scale = 1.0 / math.sqrt(row_count * devices)
    tile_y = lax.axis_index(TY)
    tile_x = lax.axis_index(TX)

    def on_raster(cells, margin):
        rows = tile_y * height - margin + jnp.arange(cells.shape[0])
        cols = tile_x * tile_width - margin + jnp.arange(cells.shape[1])
        ok_rows = (rows >= 0) & (rows < tiles_y * height)
        ok_cols = (cols >= 0) & (cols < tiles_x * tile_width)
        return jnp.where((ok_rows[:, None] & ok_cols[None, :])[:, :, None], cells, 0.0)

    margin = STEPS * REACH
    field = on_raster(0.1 + with_halo(start_field, margin, tiles_y, tiles_x), margin)
    stored = []
    for step in range(STEPS):
        margin -= REACH
        mid_value = disperse_valid(field, taps_y, taps_x)
        stored.append(mid_value)
        field = mid_value * (1.0 + rate) / (1.0 + rate * mid_value / capacity)
        if margin:
            field = on_raster(field, margin)
    grad_field = (
        surveyed[:, :, None].astype(F32) * (1.0 - observed.astype(F32) / field) * scale
    )

    def grown(grad, step, margin):
        mid_value = crop(stored[step], (STEPS - 1 - step) * REACH - margin)
        denom = 1.0 + rate * mid_value / capacity
        return grad * (1.0 + rate) / (denom * denom)

    for step in range(STEPS - 1, 0, -2):
        wide = with_halo(grown(grad_field, step, 0), 2 * REACH, tiles_y, tiles_x)
        grad_field = disperse_valid(wide, back_y, back_x)
        grad_mid = on_raster(grown(grad_field, step - 1, REACH), REACH)
        grad_field = disperse_valid(grad_mid, back_y, back_x)

    take = (cell_list[:, None] == cell_ids[None, :]).astype(BF16)
    back_values = jnp.dot(
        take, grad_field.reshape(cell_count, species).astype(BF16), preferred_element_type=F32
    ).astype(BF16)
    home_values = lax.all_to_all(
        back_values.reshape(devices, slot_count, species),
        ALL,
        split_axis=0,
        concat_axis=0,
        tiled=True,
    )
    unpack = (flat_slot[:, None] == slot_ids[None, :]).astype(BF16)
    returned = jnp.dot(unpack, home_values.reshape(slots, species), preferred_element_type=F32)
    dlog = (returned * intensity).astype(BF16)
    dhidden = lax.dot_general(dlog, w_out, (((1,), (1,)), ((), ())), preferred_element_type=F32)
    dpre = (dhidden * silu_slope(preact)).astype(BF16)
    grad_w_out = reduce_scatter(
        lax.dot_general(hidden, dlog, (((0,), (0,)), ((), ())), preferred_element_type=F32)
    )
    grad_w_in = reduce_scatter(
        lax.dot_general(covariates, dpre, (((0,), (0,)), ((), ())), preferred_element_type=F32)
    )
    return (field, grad_w_in, grad_w_out)


def solution(mesh):
    tiles_y, tiles_x = mesh.devices.shape
    split = Mesh(mesh.devices.reshape(tiles_y // 2, 2, tiles_x // 4, 4), ALL)
    in_specs = (
        P(ALL, None),
        P(),
        P(),
        P(),
        P(),
        P(ALL, None),
        P(ALL),
        P(),
        P(),
        P(),
        P(),
        P(TY, TX, None),
        P(TY, TX),
    )
    out_specs = (P(TY, TX, None), P(ALL, None), P(ALL, None))
    return jax.shard_map(local, mesh=split, in_specs=in_specs, out_specs=out_specs, check_vma=False)
```

time: 1150 us -> 316 us (0.27)
  waiting for transfers between devices: 872 us -> 82.4 us
  starting transfers between devices: 121 us -> 83.5 us
  local copies, waits for them, and re-layouts: 40.7 us -> 13.5 us
  matrix products: 39.1 us -> 65.3 us
  between operations: 15 us -> 1.73 us
    reduce_scatter x1 -> x0, waiting for transfers between devices: 638 us -> none  [local(): lax.psum_scatter(lax.dot_general(piece, dlog, (((0,), (0,)), ((), ())), p...]
    unnamed x3 -> x0, waiting for transfers between devices: 139 us -> none
    ppermute x32 -> x14, starting transfers between devices: 86.6 us -> 39.5 us  [the longest x12 38.9 us: shift(): return lax.ppermute(cells, axes, pairs)]
    ppermute x32 -> x14, waiting for transfers between devices: 59 us -> 12.1 us  [the longest x12 10.2 us: shift(): return lax.ppermute(cells, axes, pairs)]
    all_to_all x3 -> x4, waiting for transfers between devices: 35.7 us -> 70.3 us  [the longest x2 34.2 us: reduce_scatter(): return jnp.sum(lax.all_to_all(both, ('y', 'z', 'x'), 0, 0), axis=0)]
    dot_general x4 -> x11, matrix products: 39.1 us -> 65.3 us  [the longest x1 13.2 us: local(): lax.dot_general(dlog, w_out, (((1,), (1,)), ((), ())), preferred_element_...]
    gather x2 -> x0, local copies, waits for them, and re-layouts: 23.1 us -> none  [the longest x1 15 us: local(): jnp.take(grad_field.reshape(cell_count, species), cell_list, axis=0, mode...]
    scatter-add x1 -> x0, other arithmetic: 23 us -> none  [local(): start_field = jnp.zeros((cell_count, species), jnp.float32).at[cell_list]...]
  transfers between devices with their start and end apart: 37 -> 18, of which waited for: 28 -> 14; matrix products, arithmetic and copies ran while one was open for 3% -> 6% of each run, Pallas kernels for 0% -> 0%
where the time goes in v1:
time: 316 us; the launch traced here: 310 us
  starting transfers between devices  83.5 us (26%)
  waiting for transfers between devices  82.4 us (26%)
  matrix products  65.3 us (21%)
  other arithmetic  64 us (20%)
  local copies, waits for them, and re-layouts  13.5 us (4%)
    ppermute x12, starting transfers between devices, shift(): return lax.ppermute(cells, axes, pairs)  38.9 us
    all_to_all x2, waiting for transfers between devices, reduce_scatter(): return jnp.sum(lax.all_to_all(both, ('y', 'z', 'x'), 0, 0), axis=0)  34.2 us
    add x8, other arithmetic, disperse_valid(): partial_rows + taps_y[:, offset] * padded[offset:offset + height]  23.8 us
    all_to_all x1, starting transfers between devices, local(): lax.all_to_all(back_values.reshape(devices, slot_count, species), ALL, sp...  21.5 us
    all_to_all x1, waiting for transfers between devices, local(): lax.all_to_all(back_values.reshape(devices, slot_count, species), ALL, sp...  18.6 us
    all_to_all x1, waiting for transfers between devices, local(): got = lax.all_to_all(send, ALL, split_axis=0, concat_axis=0, tiled=True)  17.5 us
    select_n x6, other arithmetic, on_raster(): jnp.where((ok_rows[:, None] & ok_cols[None, :])[:, :, None], cells, 0.0)  16.7 us
    dot_general x1, matrix products, local(): lax.dot_general(dlog, w_out, (((1,), (1,)), ((), ())), preferred_element_...  13.2 us
  transfers between devices with their start and end apart: 18, of which 14 were waited for; matrix products, arithmetic and copies ran while one was open for 6% of the time, Pallas kernels for 0%

profile of v1, /device:TPU:0, one launch (start us, length us, event | category | flops | bytes accessed | tf_op | source)
XLA Modules:
  0.0 310.3 jit_solution(11331256605033515919)
XLA Ops:
  6.0 11.0 %fusion.11 = (bf16[2048,2048]{1,0:T(8,128)(2,1)S(1)}, f32[2048,2048]{1,0:T(8,128)}) fusion(f32[2048]{0:T(1024)S(1)} %copy-done.23, bf16[2048,512]{1,0:T(8,128)(2,1)S(1)} %copy-done, bf16[512,2048]{1,0:T(8,128)(2,1)} %param.14), kind=kOutput, calls=%fused_computation.18 | convolution fusion | flops 4320133120 | bytes 29368320 | tf_op jit(solution)/shard_map/dot_general | solution.py:102
  22.8 6.0 %fusion.13 = bf16[4096,128]{1,0:T(8,128)(2,1)S(1)} fusion(s32[2048]{0:T(1024)S(1)} %multiply_add_fusion.2, f32[2048,128]{1,0:T(8,128)S(1)} %fusion.42), kind=kOutput, calls=%fused_computation.20 | convolution fusion | flops 2156658688 | bytes 2105344 | tf_op jit(solution)/shard_map/dot_general | solution.py:118
  30.1 11.4 %all-to-all-start = ((bf16[128,40,128]{2,1,0:T(8,128)(2,1)}), bf16[128,40,128]{2,1,0:T(8,128)(2,1)S(1)}, u32[]{:S(2)}, u32[]{:S(2)}) async-start(bf16[128,40,128]{2,1,0:T(8,128)(2,1)} %fusion.109), calls=%async_computation | async-start | bytes 2621440 | tf_op jit(solution)/shard_map/all_to_all | solution.py:130
  45.8 17.5 %all-to-all-done = bf16[128,40,128]{2,1,0:T(8,128)(2,1)S(1)} async-done(((bf16[128,40,128]{2,1,0:T(8,128)(2,1)}), bf16[128,40,128]{2,1,0:T(8,128)(2,1)S(1)}, u32[]{:S(2)}, u32[]{:S(2)}) %all-to-all-start) | async-done | bytes 1310752 | tf_op jit(solution)/shard_map/all_to_all | solution.py:130
  65.0 4.9 %fusion.192 = (bf16[16,128,128]{2,1,0:T(8,128)(2,1)S(1)}, f32[16,128,128]{2,1,0:T(8,128)S(1)}) fusion(bf16[4096,128,1]{1,0,2:T(8,128)(2,1)S(1)} %bitcast.79, s32[16,128]{1,0:T(8,128)S(1)} %copy-done.17, s32[4096]{0:T(1024)S(1)} %copy-done.14), kind=kOutput, calls=%fused_computation.416 | convolution fusion | flops 2156134400 | bytes 2646016 | tf_op jit(solution)/shard_map/dot_general | solution.py:137
  77.3 4.6 %collective-permute-start.2 = (bf16[48,16,128]{2,1,0:T(8,128)(2,1)S(1)}, bf16[48,16,128]{2,1,0:T(8,128)(2,1)S(1)}, u32[]{:S(2)}, u32[]{:S(2)}) collective-permute-start(bf16[48,16,128]{2,1,0:T(8,128)(2,1)S(1)} %get-tuple-element.14), channel_id=1, source_target_pairs={{0,1},{1,2},{2,3},{3,4},{4,5},{5,6},{6,7},{7,8},{8,9},{9,10},{10,1... | collective-permute-start | bytes 589832 | tf_op jit(solution)/shard_map/ppermute | solution.py:22
  87.2 3.4 %fusion.15 = f32[40,160,128]{2,1,0:T(8,128)S(1)} fusion(f32[48,160,128]{2,1,0:T(8,128)S(1)} %fusion.14, f32[128]{0:T(128)S(1)} %get-tuple-element.34, f32[128]{0:T(128)S(1)} %get-tuple-element.35, f32[128]{0:T(128)S(1)} %get-tuple-element.36, f32[128]{0:T(128)S(1)} %get-tuple-element.37, f32[128]{0:T(128)S(1)} %get-tuple-element.38, ...), kind=kLoop, calls=%fused_computation.24 | loop fusion | flops 13926400 | bytes 32772608 | tf_op jit(solution)/shard_map/add | solution.py:50
  90.7 4.3 %divide_select_fusion = (f32[40,152,128]{2,1,0:T(8,128)S(1)}, f32[40,152,128]{2,1,0:T(8,128)S(1)}) fusion(f32[128]{0:T(128)S(1)} %copy-done.7, f32[128]{0:T(128)S(1)} %copy-done.6, f32[128]{0:T(128)S(1)} %get-tuple-element.46, pred[40,152]{1,0:T(8,128)(4,1)S(1)} %broadcast_and_fusion.1, f32[40,160,128]{2,1,0:T(8,128)S(1)} %fusion.15, ...), kind=kLoop, calls=%fused_computation.57 | loop fusion | flops 17899520 | bytes 34254784 | tf_op jit(solution)/shard_map/jit(_where)/select_n | solution.py:153
  108.3 6.4 %collective-permute-start.4 = (bf16[8,128,128]{2,1,0:T(8,128)(2,1)S(1)}, bf16[8,128,128]{2,1,0:T(8,128)(2,1)S(1)}, u32[]{:S(2)}, u32[]{:S(2)}) collective-permute-start(bf16[8,128,128]{2,1,0:T(8,128)(2,1)S(1)} %get-tuple-element.22), channel_id=1, source_target_pairs={{0,16},{16,32},{32,48},{48,64},{64,80},{80,96},{96,112},{1,17},{17... | collective-permute-start | bytes 786440 | tf_op jit(solution)/shard_map/ppermute | solution.py:22
  117.2 4.7 %collective-permute-start.6 = (bf16[32,8,128]{2,1,0:T(8,128)(2,1)S(1)}, bf16[32,8,128]{2,1,0:T(8,128)(2,1)S(1)}, u32[]{:S(2)}, u32[]{:S(2)}) collective-permute-start(bf16[32,8,128]{2,1,0:T(8,128)(2,1)S(1)} %get-tuple-element.18), channel_id=1, source_target_pairs={{0,1},{1,2},{2,3},{3,4},{4,5},{5,6},{6,7},{7,8},{8,9},{9,10},{10,1... | collective-permute-start | bytes 196616 | tf_op jit(solution)/shard_map/ppermute | solution.py:22
  131.3 7.8 %collective-permute-start.8 = (bf16[8,128,128]{2,1,0:T(8,128)(2,1)S(1)}, bf16[8,128,128]{2,1,0:T(8,128)(2,1)S(1)}, u32[]{:S(2)}, u32[]{:S(2)}) collective-permute-start(bf16[8,128,128]{2,1,0:T(8,128)(2,1)S(1)} %get-tuple-element.20), channel_id=1, source_target_pairs={{0,16},{16,32},{32,48},{48,64},{64,80},{80,96},{96,112},{1,17},{17... | collective-permute-start | bytes 786440 | tf_op jit(solution)/shard_map/ppermute | solution.py:22
  141.5 4.6 %collective-permute-start.10 = (bf16[32,8,128]{2,1,0:T(8,128)(2,1)S(1)}, bf16[32,8,128]{2,1,0:T(8,128)(2,1)S(1)}, u32[]{:S(2)}, u32[]{:S(2)}) collective-permute-start(bf16[32,8,128]{2,1,0:T(8,128)(2,1)S(1)} %get-tuple-element.16), channel_id=1, source_target_pairs={{0,1},{1,2},{2,3},{3,4},{4,5},{5,6},{6,7},{7,8},{8,9},{9,10},{10,1... | collective-permute-start | bytes 196616 | tf_op jit(solution)/shard_map/ppermute | solution.py:22
  148.2 13.5 %fusion.52 = f32[24,144,128]{2,1,0:T(8,128)S(1)} fusion(f32[32,144,128]{2,1,0:T(8,128)S(1)} %pad_maximum_fusion.1, f32[128]{0:T(128)S(1)} %get-tuple-element.34, f32[128]{0:T(128)S(1)} %get-tuple-element.35, f32[128]{0:T(128)S(1)} %get-tuple-element.36, f32[128]{0:T(128)S(1)} %get-tuple-element.37, f32[128]{0:T(128)S(1)} %get-tuple-element.38, ...), kind=kLoop, calls=%fused_computation.105 | loop fusion | flops 7520256 | bytes 17699328 | tf_op jit(solution)/shard_map/add | solution.py:50
  165.8 7.2 %fusion.12 = bf16[4096,128]{1,0:T(8,128)(2,1)} fusion(bf16[2048,128]{1,0:T(8,128)(2,1)S(1)} %bitcast.82, s32[4096]{0:T(1024)S(1)} %copy-done.14), kind=kOutput, calls=%fused_computation.19 | convolution fusion | flops 2156396544 | bytes 1589248 | tf_op jit(solution)/shard_map/dot_general | solution.py:181
  173.0 21.5 %all-to-all-start.1 = ((bf16[128,32,128]{2,1,0:T(8,128)(2,1)}), bf16[128,32,128]{2,1,0:T(8,128)(2,1)}, u32[]{:S(2)}, u32[]{:S(2)}) async-start(bf16[128,32,128]{2,1,0:T(8,128)(2,1)} %bitcast.78), calls=%async_computation.1 | async-start | bytes 2097152 | tf_op jit(solution)/shard_map/all_to_all | solution.py:184
  194.6 18.6 %all-to-all-done.1 = bf16[128,32,128]{2,1,0:T(8,128)(2,1)} async-done(((bf16[128,32,128]{2,1,0:T(8,128)(2,1)}), bf16[128,32,128]{2,1,0:T(8,128)(2,1)}, u32[]{:S(2)}, u32[]{:S(2)}) %all-to-all-start.1) | async-done | bytes 1048608 | tf_op jit(solution)/shard_map/all_to_all | solution.py:184
  213.2 7.6 %fusion.43 = bf16[2048,128]{1,0:T(8,128)(2,1)S(1)} fusion(f32[2048,128]{1,0:T(8,128)} %copy-done.27, bf16[4096,128]{1,0:T(8,128)(2,1)} %bitcast.27, s32[2048]{0:T(1024)S(1)} %bitcast.87), kind=kOutput, calls=%fused_computation.81 | convolution fusion | flops 2156396544 | bytes 2629632 | tf_op jit(solution)/shard_map/dot_general | solution.py:192
  220.8 13.2 %multiply_convert_fusion = bf16[2048,2048]{1,0:T(8,128)(2,1)} fusion(f32[2048,2048]{1,0:T(8,128)} %get-tuple-element.49, bf16[2048,128]{1,0:T(8,128)(2,1)S(1)} %fusion.43, bf16[2048,128]{1,0:T(8,128)(2,1)S(1)} %copy-done.22, f32[2048]{0:T(1024)S(1)} %copy-done.24), kind=kOutput, calls=%fused_computation.8 | convolution fusion | flops 1115684864 | bytes 26222592 | tf_op jit(solution)/shard_map/dot_general | solution.py:194
  234.0 6.9 %fusion.193 = f32[2048,512]{0,1:T(8,128)S(1)} fusion(bf16[2048,2048]{1,0:T(8,128)(2,1)} %multiply_convert_fusion, bf16[2048,512]{1,0:T(8,128)(2,1)S(1)} %copy-done), kind=kOutput, calls=%fused_computation.417 | convolution fusion | flops 4294967296 | bytes 14680064 | tf_op jit(solution)/shard_map/dot_general | solution.py:200
  252.5 5.5 %all-to-all-start.3 = ((f32[64,16,128]{2,1,0:T(8,128)}), f32[64,16,128]{2,1,0:T(8,128)}, u32[]{:S(2)}, u32[]{:S(2)}) async-start(f32[64,16,128]{2,1,0:T(8,128)} %bitcast.76), calls=%async_computation.3 | async-start | bytes 1048576 | tf_op jit(solution)/shard_map/all_to_all | solution.py:76
  258.0 4.0 %bitcast_add_fusion = f32[4,64,2048]{2,1,0:T(8,128)} fusion(f32[4,64,2048]{2,1,0:T(8,128)} %collective-permute-done.12, f32[4,2,64,2048]{3,2,1,0:T(8,128)} %bitcast.75, s32[]{:T(128)S(6)} %select_n.79), kind=kLoop, calls=%fused_computation.102 | loop fusion | flops 524288 | bytes 6291460 | tf_op jit(solution)/shard_map/add | solution.py:74
  264.9 7.3 %all-to-all-done.3 = f32[64,16,128]{2,1,0:T(8,128)} async-done(((f32[64,16,128]{2,1,0:T(8,128)}), f32[64,16,128]{2,1,0:T(8,128)}, u32[]{:S(2)}, u32[]{:S(2)}) %all-to-all-start.3) | async-done | bytes 524320 | tf_op jit(solution)/shard_map/all_to_all | solution.py:76
  272.1 5.6 %all-to-all-start.2 = ((f32[64,4,2048]{2,1,0:T(4,128)}), f32[64,4,2048]{2,1,0:T(4,128)}, u32[]{:S(2)}, u32[]{:S(2)}) async-start(f32[64,4,2048]{2,1,0:T(4,128)} %reshape.324), calls=%async_computation.2 | async-start | bytes 4194304 | tf_op jit(solution)/shard_map/all_to_all | solution.py:76
  280.6 27.0 %all-to-all-done.2 = f32[64,4,2048]{2,1,0:T(4,128)} async-done(((f32[64,4,2048]{2,1,0:T(4,128)}), f32[64,4,2048]{2,1,0:T(4,128)}, u32[]{:S(2)}, u32[]{:S(2)}) %all-to-all-start.2) | async-done | bytes 2097184 | tf_op jit(solution)/shard_map/all_to_all | solution.py:76
  (159 shorter events, 84.3 us)
Async XLA Ops:
  6.0 14.3 %copy-start.21 = (bf16[2048,128]{1,0:T(8,128)(2,1)S(1)}, bf16[2048,128]{1,0:T(8,128)(2,1)}, u32[]{:S(2)}) copy-start(bf16[2048,128]{1,0:T(8,128)(2,1)} %param.16) | copy-start | bytes 1572868
  6.0 14.3 %copy-start.25 = (f32[128]{0:T(128)S(1)}, f32[128]{0:T(128)}, u32[]{:S(2)}) copy-start(f32[128]{0:T(128)} %param.17) | copy-start | bytes 1540
  30.1 14.3 %copy-start.13 = (f32[128,9]{0,1:T(8,128)S(1)}, f32[128,9]{0,1:T(8,128)}, u32[]{:S(2)}) copy-start(f32[128,9]{0,1:T(8,128)} %param.21) | copy-start | bytes 13828
  30.1 33.1 %all-to-all-start = ((bf16[128,40,128]{2,1,0:T(8,128)(2,1)}), bf16[128,40,128]{2,1,0:T(8,128)(2,1)S(1)}, u32[]{:S(2)}, u32[]{:S(2)}) async-start(bf16[128,40,128]{2,1,0:T(8,128)(2,1)} %fusion.109), calls=%async_computation | async-start | bytes 2621440 | tf_op jit(solution)/shard_map/all_to_all | solution.py:130
  70.0 4.6 %collective-permute-start.1 = (bf16[16,128,128]{2,1,0:T(8,128)(2,1)S(1)}, bf16[16,128,128]{2,1,0:T(8,128)(2,1)S(1)}, u32[]{:S(2)}, u32[]{:S(2)}) collective-permute-start(bf16[16,128,128]{2,1,0:T(8,128)(2,1)S(1)} %get-tuple-element.50), channel_id=1, source_target_pairs={{16,0},{32,16},{48,32},{64,48},{80,64},{96,80},{112,96},{17,1},{33... | collective-permute-start | bytes 1572872 | tf_op jit(solution)/shard_map/ppermute | solution.py:22
  71.3 4.6 %collective-permute-start = (bf16[16,128,128]{2,1,0:T(8,128)(2,1)S(1)}, bf16[16,128,128]{2,1,0:T(8,128)(2,1)S(1)}, u32[]{:S(2)}, u32[]{:S(2)}) collective-permute-start(bf16[16,128,128]{2,1,0:T(8,128)(2,1)S(1)} %get-tuple-element.50), channel_id=1, source_target_pairs={{0,16},{16,32},{32,48},{48,64},{64,80},{80,96},{96,112},{1,17},{17... | collective-permute-start | bytes 1572872 | tf_op jit(solution)/shard_map/ppermute | solution.py:22
  76.0 7.6 %collective-permute-start.3 = (bf16[48,16,128]{2,1,0:T(8,128)(2,1)S(1)}, bf16[48,16,128]{2,1,0:T(8,128)(2,1)S(1)}, u32[]{:S(2)}, u32[]{:S(2)}) collective-permute-start(bf16[48,16,128]{2,1,0:T(8,128)(2,1)S(1)} %get-tuple-element.15), channel_id=1, source_target_pairs={{1,0},{2,1},{3,2},{4,3},{5,4},{6,5},{7,6},{8,7},{9,8},{10,9},{11,1... | collective-permute-start | bytes 589832 | tf_op jit(solution)/shard_map/ppermute | solution.py:22
  77.3 7.7 %collective-permute-start.2 = (bf16[48,16,128]{2,1,0:T(8,128)(2,1)S(1)}, bf16[48,16,128]{2,1,0:T(8,128)(2,1)S(1)}, u32[]{:S(2)}, u32[]{:S(2)}) collective-permute-start(bf16[48,16,128]{2,1,0:T(8,128)(2,1)S(1)} %get-tuple-element.14), channel_id=1, source_target_pairs={{0,1},{1,2},{2,3},{3,4},{4,5},{5,6},{6,7},{7,8},{8,9},{9,10},{10,1... | collective-permute-start | bytes 589832 | tf_op jit(solution)/shard_map/ppermute | solution.py:22
  107.0 7.7 %collective-permute-start.5 = (bf16[8,128,128]{2,1,0:T(8,128)(2,1)S(1)}, bf16[8,128,128]{2,1,0:T(8,128)(2,1)S(1)}, u32[]{:S(2)}, u32[]{:S(2)}) collective-permute-start(bf16[8,128,128]{2,1,0:T(8,128)(2,1)S(1)} %get-tuple-element.23), channel_id=1, source_target_pairs={{16,0},{32,16},{48,32},{64,48},{80,64},{96,80},{112,96},{17,1},{33... | collective-permute-start | bytes 786440 | tf_op jit(solution)/shard_map/ppermute | solution.py:22
  108.3 7.6 %collective-permute-start.4 = (bf16[8,128,128]{2,1,0:T(8,128)(2,1)S(1)}, bf16[8,128,128]{2,1,0:T(8,128)(2,1)S(1)}, u32[]{:S(2)}, u32[]{:S(2)}) collective-permute-start(bf16[8,128,128]{2,1,0:T(8,128)(2,1)S(1)} %get-tuple-element.22), channel_id=1, source_target_pairs={{0,16},{16,32},{32,48},{48,64},{64,80},{80,96},{96,112},{1,17},{17... | collective-permute-start | bytes 786440 | tf_op jit(solution)/shard_map/ppermute | solution.py:22
  115.9 6.3 %collective-permute-start.7 = (bf16[32,8,128]{2,1,0:T(8,128)(2,1)S(1)}, bf16[32,8,128]{2,1,0:T(8,128)(2,1)S(1)}, u32[]{:S(2)}, u32[]{:S(2)}) collective-permute-start(bf16[32,8,128]{2,1,0:T(8,128)(2,1)S(1)} %get-tuple-element.19), channel_id=1, source_target_pairs={{1,0},{2,1},{3,2},{4,3},{5,4},{6,5},{7,6},{8,7},{9,8},{10,9},{11,1... | collective-permute-start | bytes 196616 | tf_op jit(solution)/shard_map/ppermute | solution.py:22
  117.2 6.6 %collective-permute-start.6 = (bf16[32,8,128]{2,1,0:T(8,128)(2,1)S(1)}, bf16[32,8,128]{2,1,0:T(8,128)(2,1)S(1)}, u32[]{:S(2)}, u32[]{:S(2)}) collective-permute-start(bf16[32,8,128]{2,1,0:T(8,128)(2,1)S(1)} %get-tuple-element.18), channel_id=1, source_target_pairs={{0,1},{1,2},{2,3},{3,4},{4,5},{5,6},{6,7},{7,8},{8,9},{9,10},{10,1... | collective-permute-start | bytes 196616 | tf_op jit(solution)/shard_map/ppermute | solution.py:22
  130.0 9.1 %collective-permute-start.9 = (bf16[8,128,128]{2,1,0:T(8,128)(2,1)S(1)}, bf16[8,128,128]{2,1,0:T(8,128)(2,1)S(1)}, u32[]{:S(2)}, u32[]{:S(2)}) collective-permute-start(bf16[8,128,128]{2,1,0:T(8,128)(2,1)S(1)} %get-tuple-element.21), channel_id=1, source_target_pairs={{16,0},{32,16},{48,32},{64,48},{80,64},{96,80},{112,96},{17,1},{33... | collective-permute-start | bytes 786440 | tf_op jit(solution)/shard_map/ppermute | solution.py:22
  131.3 8.9 %collective-permute-start.8 = (bf16[8,128,128]{2,1,0:T(8,128)(2,1)S(1)}, bf16[8,128,128]{2,1,0:T(8,128)(2,1)S(1)}, u32[]{:S(2)}, u32[]{:S(2)}) collective-permute-start(bf16[8,128,128]{2,1,0:T(8,128)(2,1)S(1)} %get-tuple-element.20), channel_id=1, source_target_pairs={{0,16},{16,32},{32,48},{48,64},{64,80},{80,96},{96,112},{1,17},{17... | collective-permute-start | bytes 786440 | tf_op jit(solution)/shard_map/ppermute | solution.py:22
  140.2 6.2 %collective-permute-start.11 = (bf16[32,8,128]{2,1,0:T(8,128)(2,1)S(1)}, bf16[32,8,128]{2,1,0:T(8,128)(2,1)S(1)}, u32[]{:S(2)}, u32[]{:S(2)}) collective-permute-start(bf16[32,8,128]{2,1,0:T(8,128)(2,1)S(1)} %get-tuple-element.17), channel_id=1, source_target_pairs={{1,0},{2,1},{3,2},{4,3},{5,4},{6,5},{7,6},{8,7},{9,8},{10,9},{11,1... | collective-permute-start | bytes 196616 | tf_op jit(solution)/shard_map/ppermute | solution.py:22
  141.5 6.5 %collective-permute-start.10 = (bf16[32,8,128]{2,1,0:T(8,128)(2,1)S(1)}, bf16[32,8,128]{2,1,0:T(8,128)(2,1)S(1)}, u32[]{:S(2)}, u32[]{:S(2)}) collective-permute-start(bf16[32,8,128]{2,1,0:T(8,128)(2,1)S(1)} %get-tuple-element.16), channel_id=1, source_target_pairs={{0,1},{1,2},{2,3},{3,4},{4,5},{5,6},{6,7},{7,8},{8,9},{9,10},{10,1... | collective-permute-start | bytes 196616 | tf_op jit(solution)/shard_map/ppermute | solution.py:22
  173.0 21.6 %copy-start.11 = (s32[2048,1]{0,1:T(1,128)S(1)}, s32[2048,1]{0,1:T(1,128)}, u32[]{:S(2)}) copy-start(s32[2048,1]{0,1:T(1,128)} %param.18) | copy-start | bytes 24580
  173.0 40.2 %all-to-all-start.1 = ((bf16[128,32,128]{2,1,0:T(8,128)(2,1)}), bf16[128,32,128]{2,1,0:T(8,128)(2,1)}, u32[]{:S(2)}, u32[]{:S(2)}) async-start(bf16[128,32,128]{2,1,0:T(8,128)(2,1)} %bitcast.78), calls=%async_computation.1 | async-start | bytes 2097152 | tf_op jit(solution)/shard_map/all_to_all | solution.py:184
  213.2 30.7 %slice-start = ((s8[8388608]{0:T(1024)(128)(4,1)}), s8[4194304]{0:T(1024)(128)(4,1)S(1)}, s32[]{:S(2)}) async-start(s8[8388608]{0:T(1024)(128)(4,1)} %bitcast.88), calls=%async_computation.4 | async-start | bytes 8388608
  220.8 23.1 %slice-start.1 = ((s8[8388608]{0:T(1024)(128)(4,1)}), s8[4194304]{0:T(1024)(128)(4,1)S(1)}, s32[]{:S(2)}) async-start(s8[8388608]{0:T(1024)(128)(4,1)} %bitcast.88), calls=%async_computation.5 | async-start | bytes 8388608
  243.6 14.4 %collective-permute-start.12 = (f32[4,64,2048]{2,1,0:T(8,128)}, f32[4,64,2048]{2,1,0:T(8,128)}, u32[]{:S(2)}, u32[]{:S(2)}) collective-permute-start(f32[4,64,2048]{2,1,0:T(8,128)} %dynamic-slice_bitcast_fusion), channel_id=1, source_target_pairs={{0,16},{16,0},{1,17},{17,1},{2,18},{18,2},{3,19},{19,3},{4,20},{20... | collective-permute-start | bytes 6291464 | tf_op jit(solution)/shard_map/ppermute | solution.py:74
  248.1 2.4 collective-permute-start.13
  252.5 19.6 %all-to-all-start.3 = ((f32[64,16,128]{2,1,0:T(8,128)}), f32[64,16,128]{2,1,0:T(8,128)}, u32[]{:S(2)}, u32[]{:S(2)}) async-start(f32[64,16,128]{2,1,0:T(8,128)} %bitcast.76), calls=%async_computation.3 | async-start | bytes 1048576 | tf_op jit(solution)/shard_map/all_to_all | solution.py:76
  272.1 35.4 %all-to-all-start.2 = ((f32[64,4,2048]{2,1,0:T(4,128)}), f32[64,4,2048]{2,1,0:T(4,128)}, u32[]{:S(2)}, u32[]{:S(2)}) async-start(f32[64,4,2048]{2,1,0:T(4,128)} %reshape.324), calls=%async_computation.2 | async-start | bytes 4194304 | tf_op jit(solution)/shard_map/all_to_all | solution.py:76
  (24 other events, 115.7 us)
